TPU v7x, 32 devices: a whole 2x2x4 slice. The times are simulated.
32 devices in a mesh: grp: 2 (over x), exp: 16 (over z, y, core).
Axes of the slice: x: 2, y: 2, z: 4, core: 2. Of those that a mesh axis runs over, the one named last changes fastest.
Arguments:
- hidden: bfloat16 [32, 4096], P(('grp', 'exp')), may hold values from -6 to 6
- route_ids: int32 [32, 8], P(('grp', 'exp')), may hold values from 0 to 15, all different within a row; in each aligned block of 32 rows (0 to 31, 32 to 63, ...) at most 32 rows name the same one
- route_logits: bfloat16 [32, 8], P(('grp', 'exp')), may hold values from -6 to 6
- sampled: int32 [32], P(('grp', 'exp')), may hold values from 0 to 131071
- norm_gain: float32 [4096], replicated, may hold values from 0.5 to 1.5
- gate_weight: bfloat16 [16, 4096, 1536], P('exp', 'grp'), may hold values from -0.09375 to 0.09375
- up_weight: bfloat16 [16, 4096, 1536], P('exp', 'grp'), may hold values from -0.09375 to 0.09375
- down_weight: bfloat16 [16, 1536, 4096], P('exp', None, 'grp'), may hold values from -0.15625 to 0.15625
- head_weight: bfloat16 [4096, 131072], P(None, ('grp', 'exp')), may hold values from -0.25 to 0.25
- noise_steps: int32 [131072], P(('grp', 'exp')), may hold values from -64 to 64
Outputs:
- vote_counts: float32 [131072], P(('grp', 'exp'))
- log_ratio: float32 [32], P(('grp', 'exp'))
Inputs may be any that keep to these rules, and one draw needn't show every extreme that they name: `route_ids`: each row names 8 different experts. Over all 32 rows no expert is named by more than 32 rows, a bound that some block reaches.
All inputs are finite; a program needn't handle non-finite values.
Results may differ from a plain program's by a relative error of at most 0.004.
Values may be sent and summed in bfloat16 or wider, within the bound.
A program may use at most 128 MiB of HBM per device.

v0:
```python
import jax
import jax.numpy as jnp
from jax import lax
from jax.sharding import PartitionSpec as P

TOPK = 8
VOCAB = 131072
clip_bound = 8.0
noise_step = 0.03125
norm_eps = 1e-06


def on_device(
    hidden,
    route_ids,
    route_logits,
    sampled,
    norm_gain,
    gate_weight,
    up_weight,
    down_weight,
    head_weight,
    noise_steps,
):
    groups = lax.axis_size("grp")
    columns_count = lax.axis_size("exp")
    width = gate_weight.shape[1]
    column_index = lax.axis_index("exp")
    device_index = lax.axis_index(("grp", "exp"))
    group_rows, group_ids, group_logits, group_sampled = (
        lax.all_gather(hidden, "exp", axis=0, tiled=True),
        lax.all_gather(route_ids, "exp", axis=0, tiled=True),
        lax.all_gather(route_logits, "exp", axis=0, tiled=True),
        lax.all_gather(sampled, "exp", axis=0, tiled=True),
    )
    row_count = group_rows.shape[0]
    topk_width = group_ids.shape[1]
    pieces = group_rows.reshape(row_count, groups, width)
    ids_spread = jnp.broadcast_to(group_ids[:, None, :], (row_count, groups, topk_width))
    logits_spread = jnp.broadcast_to(group_logits[:, None, :], (row_count, groups, topk_width))
    sampled_spread = jnp.broadcast_to(group_sampled[:, None, None], (row_count, groups, 1))
    arrived = (
        lax.all_to_all(pieces, "grp", split_axis=1, concat_axis=0, tiled=True),
        lax.all_to_all(ids_spread, "grp", split_axis=1, concat_axis=0, tiled=True),
        lax.all_to_all(logits_spread, "grp", split_axis=1, concat_axis=0, tiled=True),
        lax.all_to_all(sampled_spread, "grp", split_axis=1, concat_axis=0, tiled=True),
    )
    member_count = row_count * groups
    width_slab = arrived[0].reshape(member_count, width)
    ids_all = arrived[1].reshape(member_count, topk_width)
    logits_all = arrived[2].reshape(member_count, topk_width)
    sampled_all = arrived[3].reshape(member_count)
    members_total = width_slab.shape[0]
    capacity = min(members_total, 2 * members_total * TOPK // columns_count)
    mixing = jax.nn.softmax(logits_all.astype(jnp.float32), axis=-1)
    matches = ids_all == column_index
    chosen = jnp.any(matches, axis=1)
    share = jnp.sum(jnp.where(matches, mixing, 0.0), axis=1)
    position = jnp.cumsum(chosen.astype(jnp.int32)) - 1
    slot_index = jnp.arange(capacity, dtype=jnp.int32)
    select = ((position[None, :] == slot_index[:, None]) & chosen[None, :]).astype(jnp.bfloat16)
    picked = jnp.dot(select, width_slab, preferred_element_type=jnp.float32).astype(jnp.bfloat16)
    gate_part = jnp.dot(picked, gate_weight[0], preferred_element_type=jnp.float32)
    upward_part = jnp.dot(picked, up_weight[0], preferred_element_type=jnp.float32)
    gate_sum, upward_sum = lax.psum((gate_part, upward_part), "grp")
    active = (jax.nn.silu(gate_sum) * upward_sum).astype(jnp.bfloat16)
    output = jnp.dot(active, down_weight[0], preferred_element_type=jnp.float32).astype(
        jnp.bfloat16
    )
    spread = jnp.einsum("cm,cw->mw", select, output, preferred_element_type=jnp.float32)
    contrib = spread * share[:, None]
    moe_slab = lax.psum(contrib, "exp")
    residual = (width_slab.astype(jnp.float32) + moe_slab).astype(jnp.bfloat16)
    vocab_block = head_weight.shape[1]
    piece = lax.all_gather(residual, "grp", axis=1, tiled=True)
    scaled = (piece.astype(jnp.float32) * norm_gain[None, :]).astype(jnp.bfloat16)
    acc_logits = jnp.dot(scaled, head_weight, preferred_element_type=jnp.float32)
    acc_squares = jnp.sum(jnp.square(piece.astype(jnp.float32)), axis=1)
    model_width = norm_gain.shape[0]
    root_mean = jnp.sqrt(acc_squares / model_width + norm_eps)
    logits = acc_logits / root_mean[:, None]
    clipped = jnp.clip(logits, -clip_bound, clip_bound)
    exp_values = jnp.exp(clipped)
    first_column = device_index * vocab_block
    vocab_columns = first_column + jnp.arange(vocab_block, dtype=jnp.int32)
    owned = sampled_all[:, None] == vocab_columns[None, :]
    part_total = jnp.sum(exp_values, axis=1)
    part_chosen = jnp.sum(jnp.where(owned, clipped, 0.0), axis=1)
    totals, chosen_logit = lax.psum((part_total, part_chosen), ("grp", "exp"))
    log_ratio = chosen_logit - jnp.log(totals / VOCAB)
    own_rows = hidden.shape[0]
    own_ratio = lax.dynamic_slice_in_dim(log_ratio, device_index * own_rows, own_rows, 0)
    vote_counts = (
        VOCAB / members_total * jnp.sum(exp_values / totals[:, None], axis=0)
        + noise_steps.astype(jnp.float32) * noise_step
    )
    return (vote_counts, own_ratio)


def solution(mesh):
    placed = (
        P(("grp", "exp"), None),
        P(("grp", "exp"), None),
        P(("grp", "exp"), None),
        P(("grp", "exp")),
        P(),
        P("exp", "grp", None),
        P("exp", "grp", None),
        P("exp", None, "grp"),
        P(None, ("grp", "exp")),
        P(("grp", "exp")),
    )
    return jax.shard_map(
        on_device,
        mesh=mesh,
        in_specs=placed,
        out_specs=(P(("grp", "exp")), P(("grp", "exp"))),
        check_vma=False,
    )
```

profile of v0, /device:TPU:0, one launch (start us, length us, event | category | flops | bytes accessed | tf_op | source)
XLA Modules:
  0.0 297.2 jit_solution(6315251923228911917)
XLA Ops:
  7.2 23.3 %all-gather.1 = s32[16,1,8]{2,1,0:T(1,128)S(1)} all-gather(s32[1,1,8]{2,1,0:T(1,128)} %bitcast.59), channel_id=1, replica_groups=mesh['grp'=2,'exp'=16] {'exp'}, dimensions={0}, use_global_device_ids=true | all-gather | bytes 544 | tf_op jit(solution)/shard_map/all_gather | solution.py:32
  30.5 0.1 copy.24
  30.5 0.6 reshape.123
  31.2 3.2 %all-to-all-start.1 = ((s32[2,1,128]{2,1,0:T(1,128)}), s32[2,1,128]{2,1,0:T(1,128)S(1)}, u32[]{:S(2)}, u32[]{:S(2)}) async-start(s32[2,1,128]{2,1,0:T(1,128)} %reshape.123), calls=%async_computation.1 | async-start | bytes 2048 | tf_op jit(solution)/shard_map/all_to_all | solution.py:44
  34.4 18.4 %all-gather = bf16[16,1,4096]{2,1,0:T(2,128)(2,1)S(1)} all-gather(bf16[1,1,4096]{2,1,0:T(2,128)(2,1)} %bitcast.55), channel_id=1, replica_groups=mesh['grp'=2,'exp'=16] {'exp'}, dimensions={0}, use_global_device_ids=true | all-gather | bytes 139264 | tf_op jit(solution)/shard_map/all_gather | solution.py:31
  52.8 0.7 reduce.5
  53.5 0.6 copy.29
  54.2 0.0 all-to-all-done.1
  54.2 3.4 %all-to-all-start = ((bf16[16,2,2048]{2,0,1:T(8,128)(2,1)}), bf16[16,2,2048]{2,0,1:T(8,128)(2,1)S(1)}, u32[]{:S(2)}, u32[]{:S(2)}) async-start(bf16[16,2,2048]{2,0,1:T(8,128)(2,1)} %bitcast.52), calls=%async_computation | async-start | bytes 262144 | tf_op jit(solution)/shard_map/all_to_all | solution.py:43
  57.6 0.0 all-reduce.7.cloned.1.call-start
  57.6 0.5 broadcast.52
  58.1 0.7 reduce.8
  58.8 0.1 reshape.124
  58.9 0.1 and.12
  59.0 0.1 reshape.120
  59.1 0.1 reduce-window.8
  59.1 0.1 add_reduce_fusion
  59.2 2.9 all-to-all-done
  62.1 0.0 copy-start
  62.1 0.2 convolution_convert_fusion
  62.3 0.0 copy-start.3
  62.3 4.8 %fusion.2 = f32[32,1536]{1,0:T(8,128)} fusion(bf16[32,2048]{1,0:T(8,128)(2,1)S(1)} %convolution_convert_fusion, bf16[1,2048,1536]{2,1,0:T(8,128)(2,1)} %param.16), kind=kOutput, calls=%fused_computation.2 | convolution fusion | flops 201326592 | bytes 6619136 | tf_op jit(solution)/shard_map/dot_general | solution.py:64
  67.0 0.0 copy-done
  67.0 0.0 copy-start.4
  67.0 0.0 copy-start.1
  67.0 1.8 fusion.4
  68.9 0.0 all-reduce.7.cloned.1.call-update
  68.9 0.0 all-reduce.5.cloned.1.call-start
  68.9 0.0 copy-done.3
  68.9 19.2 %all-gather.2 = bf16[16,1,8]{2,1,0:T(2,128)(2,1)S(1)} all-gather(bf16[1,1,8]{2,1,0:T(2,128)(2,1)S(1)} %bitcast.60), channel_id=1, replica_groups=mesh['grp'=2,'exp'=16] {'exp'}, dimensions={0}, use_global_device_ids=true | all-gather | bytes 272 | tf_op jit(solution)/shard_map/all_gather | solution.py:33
  88.1 0.1 copy.26
  88.2 6.1 %all_to_all.54 = bf16[16,2,8]{0,2,1:T(8,128)(2,1)S(1)} all-to-all(bf16[16,2,8]{0,2,1:T(8,128)(2,1)S(1)} %broadcast_in_dim.13), channel_id=1, replica_groups=mesh['grp'=2,'exp'=16] {'grp'}, dimensions={1} | all-to-all | bytes 1024 | tf_op jit(solution)/shard_map/all_to_all | solution.py:45
  94.4 0.1 mul.45
  94.5 0.0 all-reduce.7.cloned.1.call-done
  94.5 5.0 %convolution_multiply_fusion = f32[32,2048]{1,0:T(8,128)} fusion(bf16[1,1536,2048]{2,1,0:T(8,128)(2,1)} %param.17, f32[32]{0:T(128)S(1)} %mul.45, f32[32,1536]{1,0:T(8,128)} %get-tuple-element.4, f32[32,1536]{1,0:T(8,128)} %get-tuple-element.5, s32[32]{0:T(128)S(1)} %add_reduce_fusion, pred[32]{0:T(512)(128)(4,1)S(1)} %and.12), kind=kOutput, calls=%fused_computation.8 | convolution fusion | flops 205948928 | bytes 6947104 | tf_op jit(solution)/shard_map/cm,cw->mw/dot_general | solution.py:70
  99.5 0.0 all-reduce.5.cloned.1.call-update
  100.2 0.0 copy-done.4
  100.2 0.6 dynamic-slice
  100.8 0.8 dynamic-update-slice
  101.5 10.2 %all-reduce = s32[16]{0:T(128)S(1)} all-reduce(s32[16]{0:T(128)S(1)} %dynamic-update-slice), channel_id=1, replica_groups=mesh['grp'=2,'exp'=16] {'exp'}, use_global_device_ids=true, to_apply=%add | all-reduce | flops 16 | bytes 128
  111.7 0.6 broadcast_in_dim.16
  112.3 3.2 %all-to-all-start.3 = ((s32[16,2,1]{0,2,1:T(1,128)}), s32[16,2,1]{0,2,1:T(1,128)S(1)}, u32[]{:S(2)}, u32[]{:S(2)}) async-start(s32[16,2,1]{0,2,1:T(1,128)} %broadcast_in_dim.16), calls=%async_computation.3 | async-start | bytes 2048 | tf_op jit(solution)/shard_map/all_to_all | solution.py:46
  115.5 3.7 %all-to-all-done.3 = s32[16,2,1]{0,2,1:T(1,128)S(1)} async-done(((s32[16,2,1]{0,2,1:T(1,128)}), s32[16,2,1]{0,2,1:T(1,128)S(1)}, u32[]{:S(2)}, u32[]{:S(2)}) %all-to-all-start.3) | async-done | bytes 160 | tf_op jit(solution)/shard_map/all_to_all | solution.py:46
  119.2 0.1 eq.49
  119.3 68.5 %all-reduce.5.cloned.1.call-done = f32[32,2048]{1,0:T(8,128)} async-done(((f32[32,2048]{1,0:T(8,128)}), f32[32,2048]{1,0:T(8,128)}) %all-reduce.5.cloned.1.call-update) | async-done | bytes 262160 | tf_op jit(solution)/shard_map/psum | solution.py:72
  187.8 1.0 add_convert_fusion
  188.8 6.5 %all_gather.18 = bf16[32,4096]{1,0:T(8,128)(2,1)S(1)} all-gather(bf16[32,2048]{1,0:T(8,128)(2,1)S(1)} %add_convert_fusion), channel_id=1, replica_groups=mesh['grp'=2,'exp'=16] {'grp'}, dimensions={1}, use_global_device_ids=true | all-gather | bytes 393216 | tf_op jit(solution)/shard_map/all_gather | solution.py:75
  195.3 0.2 fusion.13
  195.5 0.0 copy-done.1
  195.5 0.0 copy-start.2
  195.5 13.7 %exponential_reduce_fusion = (f32[32]{0:T(128)S(1)}, f32[32,4096]{1,0:T(8,128)S(1)}) fusion(f32[32]{0:T(128)S(1)} %add_sqrt_fusion, bf16[4096,4096]{1,0:T(8,128)(2,1)} %param.18, bf16[32,4096]{1,0:T(8,128)(2,1)S(1)} %all_gather.18, f32[4096]{0:T(1024)S(1)} %copy-done.1), kind=kOutput, calls=%fused_computation.17 | convolution fusion | flops 1074528256 | bytes 34357504 | tf_op jit(solution)/shard_map/dot_general | solution.py:77
  209.2 39.8 %psum.38 = f32[32]{0:T(128)S(1)} all-reduce(f32[32]{0:T(128)S(1)} %get-tuple-element.8), channel_id=1, replica_groups=mesh['grp'=2,'exp'=16] {'grp','exp'}, use_global_device_ids=true, to_apply=%region_10.11 | all-reduce | flops 32 | bytes 256 | tf_op jit(solution)/shard_map/psum | solution.py:89
  249.0 0.2 select_reduce_fusion
  249.2 39.9 %psum.39 = f32[32]{0:T(128)S(1)} all-reduce(f32[32]{0:T(128)S(1)} %get-tuple-element.2), channel_id=1, replica_groups=mesh['grp'=2,'exp'=16] {'grp','exp'}, use_global_device_ids=true, to_apply=%region_13.14 | all-reduce | flops 32 | bytes 256 | tf_op jit(solution)/shard_map/psum | solution.py:89
  289.1 0.0 copy-done.2
  289.1 0.6 multiply_add_fusion
  289.8 0.6 dynamic_slice.3
  (12 shorter events, 0.1 us)
Async XLA Ops:
  31.2 23.0 %all-to-all-start.1 = ((s32[2,1,128]{2,1,0:T(1,128)}), s32[2,1,128]{2,1,0:T(1,128)S(1)}, u32[]{:S(2)}, u32[]{:S(2)}) async-start(s32[2,1,128]{2,1,0:T(1,128)} %reshape.123), calls=%async_computation.1 | async-start | bytes 2048 | tf_op jit(solution)/shard_map/all_to_all | solution.py:44
  54.2 7.9 %all-to-all-start = ((bf16[16,2,2048]{2,0,1:T(8,128)(2,1)}), bf16[16,2,2048]{2,0,1:T(8,128)(2,1)S(1)}, u32[]{:S(2)}, u32[]{:S(2)}) async-start(bf16[16,2,2048]{2,0,1:T(8,128)(2,1)} %bitcast.52), calls=%async_computation | async-start | bytes 262144 | tf_op jit(solution)/shard_map/all_to_all | solution.py:43
  57.6 36.9 %all-reduce.7.cloned.1.call-start = ((), (), s32[]{:S(2)}) async-start(), calls=%async_computation.5 | async-start | bytes 786432 | tf_op jit(solution)/shard_map/psum | solution.py:65
  62.1 4.9 %copy-start = (bf16[1,2048,1536]{2,1,0:T(8,128)(2,1)S(1)}, bf16[1,2048,1536]{2,1,0:T(8,128)(2,1)}, u32[]{:S(2)}) copy-start(bf16[1,2048,1536]{2,1,0:T(8,128)(2,1)} %param.15) | copy-start | bytes 18874372
  62.3 6.7 %copy-start.3 = (bf16[1,8]{1,0:T(2,128)(2,1)S(1)}, bf16[1,8]{1,0:T(2,128)(2,1)}, u32[]{:S(2)}) copy-start(bf16[1,8]{1,0:T(2,128)(2,1)} %param.12) | copy-start | bytes 52
  67.0 33.1 %copy-start.4 = (u32[32]{0:T(128)S(1)}, u32[32]{0:T(128)}, u32[]{:S(2)}) copy-start(u32[32]{0:T(128)} %constant.59) | copy-start | bytes 388
  67.0 128.4 %copy-start.1 = (f32[4096]{0:T(1024)S(1)}, f32[4096]{0:T(1024)}, u32[]{:S(2)}) copy-start(f32[4096]{0:T(1024)} %param.14) | copy-start | bytes 49156
  68.9 118.9 %all-reduce.5.cloned.1.call-start = ((), (), s32[]{:S(2)}) async-start(), calls=%async_computation.4 | async-start | bytes 524288 | tf_op jit(solution)/shard_map/psum | solution.py:72
  112.3 6.9 %all-to-all-start.3 = ((s32[16,2,1]{0,2,1:T(1,128)}), s32[16,2,1]{0,2,1:T(1,128)S(1)}, u32[]{:S(2)}, u32[]{:S(2)}) async-start(s32[16,2,1]{0,2,1:T(1,128)} %broadcast_in_dim.16), calls=%async_computation.3 | async-start | bytes 2048 | tf_op jit(solution)/shard_map/all_to_all | solution.py:46
  195.5 93.7 %copy-start.2 = (s32[4096]{0:T(1024)S(1)}, s32[4096]{0:T(1024)}, u32[]{:S(2)}) copy-start(s32[4096]{0:T(1024)} %param.19) | copy-start | bytes 49156
Sparse Core Ops, SparseCore 0:
  69.0 23.5 all-reduce.6
  99.6 88.1 all-reduce.4
where the time goes:
time: 298 us; the launch traced here: 297 us
  blocking collectives  163 us (55%)
  waiting for transfers between devices  75.1 us (25%)
  matrix products  25.4 us (9%)
  between operations  14.8 us (5%)
  starting transfers between devices  9.85 us (3%)
  local copies, waits for them, and re-layouts  4.89 us (2%)
  other arithmetic  3.71 us (1%)
    psum x2, blocking collectives, on_device(): totals, chosen_logit = lax.psum((part_total, part_chosen), ('grp', 'exp'))  79.7 us
    psum x1, waiting for transfers between devices, on_device(): moe_slab = lax.psum(contrib, 'exp')  68.5 us
    all_gather x1, blocking collectives, on_device(): lax.all_gather(route_ids, 'exp', axis=0, tiled=True)  23.3 us
    all_gather x1, blocking collectives, on_device(): lax.all_gather(route_logits, 'exp', axis=0, tiled=True)  19.2 us
    all_gather x1, blocking collectives, on_device(): lax.all_gather(hidden, 'exp', axis=0, tiled=True)  18.4 us
    dot_general x1, matrix products, on_device(): jnp.dot(scaled, head_weight, preferred_element_type=jnp.float32)  13.7 us
    unnamed x1, blocking collectives  10.2 us
    all_gather x1, blocking collectives, on_device(): piece = lax.all_gather(residual, 'grp', axis=1, tiled=True)  6.51 us
  transfers between devices with their start and end apart: 5, of which 3 were waited for; matrix products, arithmetic and copies ran while one was open for 2% of the time, Pallas kernels for 0%

commit v1 on v0

--- a/solution.py
+++ b/solution.py
@@ -86,7 +86,7 @@
     owned = sampled_all[:, None] == vocab_columns[None, :]
     part_total = jnp.sum(exp_values, axis=1)
     part_chosen = jnp.sum(jnp.where(owned, clipped, 0.0), axis=1)
-    totals, chosen_logit = lax.psum((part_total, part_chosen), ("grp", "exp"))
+    totals, chosen_logit = lax.psum(lax.psum((part_total, part_chosen), "grp"), "exp")
     log_ratio = chosen_logit - jnp.log(totals / VOCAB)
     own_rows = hidden.shape[0]
     own_ratio = lax.dynamic_slice_in_dim(log_ratio, device_index * own_rows, own_rows, 0)

time: 298 us -> 287 us (0.963)
  blocking collectives: 163 us -> 152 us
    psum x2 -> x4, blocking collectives: 79.7 us -> 68.8 us  [the longest x2 58.9 us: on_device(): lax.psum(lax.psum((part_total, part_chosen), 'grp'), 'exp')]
where the time goes in v1:
time: 287 us; the launch traced here: 286 us
  blocking collectives  152 us (53%)
  waiting for transfers between devices  75.1 us (26%)
  matrix products  25.4 us (9%)
  between operations  14.8 us (5%)
  starting transfers between devices  9.85 us (3%)
  local copies, waits for them, and re-layouts  4.89 us (2%)
  other arithmetic  3.71 us (1%)
    psum x1, waiting for transfers between devices, on_device(): moe_slab = lax.psum(contrib, 'exp')  68.5 us
    psum x2, blocking collectives, on_device(): lax.psum(lax.psum((part_total, part_chosen), 'grp'), 'exp')  58.9 us
    all_gather x1, blocking collectives, on_device(): lax.all_gather(route_ids, 'exp', axis=0, tiled=True)  23.3 us
    all_gather x1, blocking collectives, on_device(): lax.all_gather(route_logits, 'exp', axis=0, tiled=True)  19.2 us
    all_gather x1, blocking collectives, on_device(): lax.all_gather(hidden, 'exp', axis=0, tiled=True)  18.4 us
    dot_general x1, matrix products, on_device(): jnp.dot(scaled, head_weight, preferred_element_type=jnp.float32)  13.7 us
    unnamed x1, blocking collectives  10.2 us
    psum x2, blocking collectives, on_device(): lax.psum((part_total, part_chosen), 'grp')  9.86 us
  transfers between devices with their start and end apart: 5, of which 3 were waited for; matrix products, arithmetic and copies ran while one was open for 2% of the time, Pallas kernels for 0%

profile of v1, /device:TPU:0, one launch (start us, length us, event | category | flops | bytes accessed | tf_op | source)
XLA Modules:
  0.0 286.3 jit_solution(1715758485845592837)
XLA Ops:
  7.2 23.3 %all-gather.1 = s32[16,1,8]{2,1,0:T(1,128)S(1)} all-gather(s32[1,1,8]{2,1,0:T(1,128)} %bitcast.59), channel_id=1, replica_groups=mesh['grp'=2,'exp'=16] {'exp'}, dimensions={0}, use_global_device_ids=true | all-gather | bytes 544 | tf_op jit(solution)/shard_map/all_gather | solution.py:32
  30.5 0.1 copy.24
  30.5 0.6 reshape.123
  31.2 3.2 %all-to-all-start.1 = ((s32[2,1,128]{2,1,0:T(1,128)}), s32[2,1,128]{2,1,0:T(1,128)S(1)}, u32[]{:S(2)}, u32[]{:S(2)}) async-start(s32[2,1,128]{2,1,0:T(1,128)} %reshape.123), calls=%async_computation.1 | async-start | bytes 2048 | tf_op jit(solution)/shard_map/all_to_all | solution.py:44
  34.4 18.4 %all-gather = bf16[16,1,4096]{2,1,0:T(2,128)(2,1)S(1)} all-gather(bf16[1,1,4096]{2,1,0:T(2,128)(2,1)} %bitcast.55), channel_id=1, replica_groups=mesh['grp'=2,'exp'=16] {'exp'}, dimensions={0}, use_global_device_ids=true | all-gather | bytes 139264 | tf_op jit(solution)/shard_map/all_gather | solution.py:31
  52.8 0.7 reduce.5
  53.5 0.6 copy.29
  54.2 0.0 all-to-all-done.1
  54.2 3.4 %all-to-all-start = ((bf16[16,2,2048]{2,0,1:T(8,128)(2,1)}), bf16[16,2,2048]{2,0,1:T(8,128)(2,1)S(1)}, u32[]{:S(2)}, u32[]{:S(2)}) async-start(bf16[16,2,2048]{2,0,1:T(8,128)(2,1)} %bitcast.52), calls=%async_computation | async-start | bytes 262144 | tf_op jit(solution)/shard_map/all_to_all | solution.py:43
  57.6 0.0 all-reduce.7.cloned.1.call-start
  57.6 0.5 broadcast.52
  58.1 0.7 reduce.8
  58.8 0.1 reshape.124
  58.9 0.1 and.12
  59.0 0.1 reshape.120
  59.1 0.1 reduce-window.8
  59.1 0.1 add_reduce_fusion
  59.2 2.9 all-to-all-done
  62.1 0.0 copy-start
  62.1 0.2 convolution_convert_fusion
  62.3 0.0 copy-start.3
  62.3 4.8 %fusion.2 = f32[32,1536]{1,0:T(8,128)} fusion(bf16[32,2048]{1,0:T(8,128)(2,1)S(1)} %convolution_convert_fusion, bf16[1,2048,1536]{2,1,0:T(8,128)(2,1)} %param.16), kind=kOutput, calls=%fused_computation.2 | convolution fusion | flops 201326592 | bytes 6619136 | tf_op jit(solution)/shard_map/dot_general | solution.py:64
  67.0 0.0 copy-done
  67.0 0.0 copy-start.4
  67.0 0.0 copy-start.1
  67.0 1.8 fusion.4
  68.9 0.0 all-reduce.7.cloned.1.call-update
  68.9 0.0 all-reduce.5.cloned.1.call-start
  68.9 0.0 copy-done.3
  68.9 19.2 %all-gather.2 = bf16[16,1,8]{2,1,0:T(2,128)(2,1)S(1)} all-gather(bf16[1,1,8]{2,1,0:T(2,128)(2,1)S(1)} %bitcast.60), channel_id=1, replica_groups=mesh['grp'=2,'exp'=16] {'exp'}, dimensions={0}, use_global_device_ids=true | all-gather | bytes 272 | tf_op jit(solution)/shard_map/all_gather | solution.py:33
  88.1 0.1 copy.26
  88.2 6.1 %all_to_all.54 = bf16[16,2,8]{0,2,1:T(8,128)(2,1)S(1)} all-to-all(bf16[16,2,8]{0,2,1:T(8,128)(2,1)S(1)} %broadcast_in_dim.13), channel_id=1, replica_groups=mesh['grp'=2,'exp'=16] {'grp'}, dimensions={1} | all-to-all | bytes 1024 | tf_op jit(solution)/shard_map/all_to_all | solution.py:45
  94.4 0.1 mul.45
  94.5 0.0 all-reduce.7.cloned.1.call-done
  94.5 5.0 %convolution_multiply_fusion = f32[32,2048]{1,0:T(8,128)} fusion(bf16[1,1536,2048]{2,1,0:T(8,128)(2,1)} %param.17, f32[32]{0:T(128)S(1)} %mul.45, f32[32,1536]{1,0:T(8,128)} %get-tuple-element.4, f32[32,1536]{1,0:T(8,128)} %get-tuple-element.5, s32[32]{0:T(128)S(1)} %add_reduce_fusion, pred[32]{0:T(512)(128)(4,1)S(1)} %and.12), kind=kOutput, calls=%fused_computation.8 | convolution fusion | flops 205948928 | bytes 6947104 | tf_op jit(solution)/shard_map/cm,cw->mw/dot_general | solution.py:70
  99.5 0.0 all-reduce.5.cloned.1.call-update
  100.2 0.0 copy-done.4
  100.2 0.6 dynamic-slice
  100.8 0.8 dynamic-update-slice
  101.5 10.2 %all-reduce = s32[16]{0:T(128)S(1)} all-reduce(s32[16]{0:T(128)S(1)} %dynamic-update-slice), channel_id=1, replica_groups=mesh['grp'=2,'exp'=16] {'exp'}, use_global_device_ids=true, to_apply=%add | all-reduce | flops 16 | bytes 128
  111.7 0.6 broadcast_in_dim.16
  112.3 3.2 %all-to-all-start.3 = ((s32[16,2,1]{0,2,1:T(1,128)}), s32[16,2,1]{0,2,1:T(1,128)S(1)}, u32[]{:S(2)}, u32[]{:S(2)}) async-start(s32[16,2,1]{0,2,1:T(1,128)} %broadcast_in_dim.16), calls=%async_computation.3 | async-start | bytes 2048 | tf_op jit(solution)/shard_map/all_to_all | solution.py:46
  115.5 3.7 %all-to-all-done.3 = s32[16,2,1]{0,2,1:T(1,128)S(1)} async-done(((s32[16,2,1]{0,2,1:T(1,128)}), s32[16,2,1]{0,2,1:T(1,128)S(1)}, u32[]{:S(2)}, u32[]{:S(2)}) %all-to-all-start.3) | async-done | bytes 160 | tf_op jit(solution)/shard_map/all_to_all | solution.py:46
  119.2 0.1 eq.49
  119.3 68.5 %all-reduce.5.cloned.1.call-done = f32[32,2048]{1,0:T(8,128)} async-done(((f32[32,2048]{1,0:T(8,128)}), f32[32,2048]{1,0:T(8,128)}) %all-reduce.5.cloned.1.call-update) | async-done | bytes 262160 | tf_op jit(solution)/shard_map/psum | solution.py:72
  187.8 1.0 add_convert_fusion
  188.8 6.5 %all_gather.18 = bf16[32,4096]{1,0:T(8,128)(2,1)S(1)} all-gather(bf16[32,2048]{1,0:T(8,128)(2,1)S(1)} %add_convert_fusion), channel_id=1, replica_groups=mesh['grp'=2,'exp'=16] {'grp'}, dimensions={1}, use_global_device_ids=true | all-gather | bytes 393216 | tf_op jit(solution)/shard_map/all_gather | solution.py:75
  195.3 0.2 fusion.13
  195.5 0.0 copy-done.1
  195.5 0.0 copy-start.2
  195.5 13.7 %exponential_reduce_fusion = (f32[32]{0:T(128)S(1)}, f32[32,4096]{1,0:T(8,128)S(1)}) fusion(f32[32]{0:T(128)S(1)} %add_sqrt_fusion, bf16[4096,4096]{1,0:T(8,128)(2,1)} %param.18, bf16[32,4096]{1,0:T(8,128)(2,1)S(1)} %all_gather.18, f32[4096]{0:T(1024)S(1)} %copy-done.1), kind=kOutput, calls=%fused_computation.17 | convolution fusion | flops 1074528256 | bytes 34357504 | tf_op jit(solution)/shard_map/dot_general | solution.py:77
  209.2 4.9 %psum.52 = f32[32]{0:T(128)S(1)} all-reduce(f32[32]{0:T(128)S(1)} %get-tuple-element.8), channel_id=1, replica_groups=mesh['grp'=2,'exp'=16] {'grp'}, use_global_device_ids=true, to_apply=%region_10.11 | all-reduce | flops 32 | bytes 256 | tf_op jit(solution)/shard_map/psum | solution.py:89
  214.1 29.5 %psum.53 = f32[32]{0:T(128)S(1)} all-reduce(f32[32]{0:T(128)S(1)} %psum.52), channel_id=1, replica_groups=mesh['grp'=2,'exp'=16] {'exp'}, use_global_device_ids=true, to_apply=%region_11.12 | all-reduce | flops 32 | bytes 256 | tf_op jit(solution)/shard_map/psum | solution.py:89
  243.6 0.2 select_reduce_fusion
  243.8 4.9 %psum.54 = f32[32]{0:T(128)S(1)} all-reduce(f32[32]{0:T(128)S(1)} %get-tuple-element.2), channel_id=1, replica_groups=mesh['grp'=2,'exp'=16] {'grp'}, use_global_device_ids=true, to_apply=%region_14.15 | all-reduce | flops 32 | bytes 256 | tf_op jit(solution)/shard_map/psum | solution.py:89
  248.7 29.5 %psum.55 = f32[32]{0:T(128)S(1)} all-reduce(f32[32]{0:T(128)S(1)} %psum.54), channel_id=1, replica_groups=mesh['grp'=2,'exp'=16] {'exp'}, use_global_device_ids=true, to_apply=%region_15.16 | all-reduce | flops 32 | bytes 256 | tf_op jit(solution)/shard_map/psum | solution.py:89
  278.2 0.0 copy-done.2
  278.2 0.6 multiply_add_fusion
  278.8 0.6 dynamic_slice.3
  (12 shorter events, 0.1 us)
Async XLA Ops:
  31.2 23.0 %all-to-all-start.1 = ((s32[2,1,128]{2,1,0:T(1,128)}), s32[2,1,128]{2,1,0:T(1,128)S(1)}, u32[]{:S(2)}, u32[]{:S(2)}) async-start(s32[2,1,128]{2,1,0:T(1,128)} %reshape.123), calls=%async_computation.1 | async-start | bytes 2048 | tf_op jit(solution)/shard_map/all_to_all | solution.py:44
  54.2 7.9 %all-to-all-start = ((bf16[16,2,2048]{2,0,1:T(8,128)(2,1)}), bf16[16,2,2048]{2,0,1:T(8,128)(2,1)S(1)}, u32[]{:S(2)}, u32[]{:S(2)}) async-start(bf16[16,2,2048]{2,0,1:T(8,128)(2,1)} %bitcast.52), calls=%async_computation | async-start | bytes 262144 | tf_op jit(solution)/shard_map/all_to_all | solution.py:43
  57.6 36.9 %all-reduce.7.cloned.1.call-start = ((), (), s32[]{:S(2)}) async-start(), calls=%async_computation.5 | async-start | bytes 786432 | tf_op jit(solution)/shard_map/psum | solution.py:65
  62.1 4.9 %copy-start = (bf16[1,2048,1536]{2,1,0:T(8,128)(2,1)S(1)}, bf16[1,2048,1536]{2,1,0:T(8,128)(2,1)}, u32[]{:S(2)}) copy-start(bf16[1,2048,1536]{2,1,0:T(8,128)(2,1)} %param.15) | copy-start | bytes 18874372
  62.3 6.7 %copy-start.3 = (bf16[1,8]{1,0:T(2,128)(2,1)S(1)}, bf16[1,8]{1,0:T(2,128)(2,1)}, u32[]{:S(2)}) copy-start(bf16[1,8]{1,0:T(2,128)(2,1)} %param.12) | copy-start | bytes 52
  67.0 33.1 %copy-start.4 = (u32[32]{0:T(128)S(1)}, u32[32]{0:T(128)}, u32[]{:S(2)}) copy-start(u32[32]{0:T(128)} %constant.59) | copy-start | bytes 388
  67.0 128.4 %copy-start.1 = (f32[4096]{0:T(1024)S(1)}, f32[4096]{0:T(1024)}, u32[]{:S(2)}) copy-start(f32[4096]{0:T(1024)} %param.14) | copy-start | bytes 49156
  68.9 118.9 %all-reduce.5.cloned.1.call-start = ((), (), s32[]{:S(2)}) async-start(), calls=%async_computation.4 | async-start | bytes 524288 | tf_op jit(solution)/shard_map/psum | solution.py:72
  112.3 6.9 %all-to-all-start.3 = ((s32[16,2,1]{0,2,1:T(1,128)}), s32[16,2,1]{0,2,1:T(1,128)S(1)}, u32[]{:S(2)}, u32[]{:S(2)}) async-start(s32[16,2,1]{0,2,1:T(1,128)} %broadcast_in_dim.16), calls=%async_computation.3 | async-start | bytes 2048 | tf_op jit(solution)/shard_map/all_to_all | solution.py:46
  195.5 82.8 %copy-start.2 = (s32[4096]{0:T(1024)S(1)}, s32[4096]{0:T(1024)}, u32[]{:S(2)}) copy-start(s32[4096]{0:T(1024)} %param.19) | copy-start | bytes 49156
Sparse Core Ops, SparseCore 0:
  69.0 23.5 all-reduce.6
  99.6 88.1 all-reduce.4
